TPU v7x, 512 devices: a whole 4x4x16 slice. The times are simulated.
512 devices in a mesh: dp: 64 (over x, y, z_hi, core), shard: 8 (over z_lo).
Axes of the slice: x: 4, y: 4, z: 16 (z_hi: 2, z_lo: 8; z = z_hi * 8 + z_lo), core: 2. Of those that a mesh axis runs over, the one named last changes fastest.
Arguments:
- group_grads: bfloat16 [64, 1024, 1024], P('dp', 'shard'), may hold values from -2 to 2
- moment: float32 [1024, 1024], P('shard'), may hold values from -6 to 6
- second: float32 [1024, 1024], P(None, 'shard'), may hold values from 0.5 to 4
- stat_left: float32 [1024, 1024], P('shard'), may hold values from -200 to 2000, as said below
- stat_right: float32 [1024, 1024], P('shard'), may hold values from -200 to 2000, as said below
- basis_left: float32 [1024, 1024], P('shard'), as said below
- basis_right: float32 [1024, 1024], P('shard'), as said below
Outputs:
- update: bfloat16 [1024, 1024], P('shard')
- second_new: float32 [1024, 1024], P(None, 'shard')
- left_new: float32 [1024, 1024], P('shard')
- right_new: float32 [1024, 1024], P('shard')
Inputs may be any that keep to these rules, and one draw needn't show every extreme that they name: `stat_left`: each statistic is symmetric. `stat_right`: each statistic is symmetric. `basis_left`: diagonal entries near 0.9 sqrt(1024), off-diagonal entries of order one. `basis_right`: diagonal entries near 0.9 sqrt(1024), off-diagonal entries of order one.
All inputs are finite; a program needn't handle non-finite values.
Results may differ from a plain program's by a relative error of at most 0.0049.
The roundings to bfloat16 on the way count: a program that leaves them out, or rounds other values in their place, can miss the bound.
Values may be sent and summed in bfloat16 or wider, within the bound.
A program may use at most 128 MiB of HBM per device.

v0:
```python
import jax
import jax.numpy as jnp
from jax import lax
from jax.sharding import PartitionSpec as P

NS_ITERS = 2
BETA_ONE = 0.9
BETA_TWO = 0.9
BETA_STAT = 0.95
EPSILON = 1e-08
NORM_EPS = 1e-06


def contract_rows(left_mat, right_mat):
    return lax.dot_general(
        left_mat, right_mat, (((0,), (0,)), ((), ())), preferred_element_type=jnp.float32
    )


def contract_cols(left_mat, right_mat):
    return lax.dot_general(
        left_mat, right_mat, (((1,), (1,)), ((), ())), preferred_element_type=jnp.float32
    )


def body(group_grads, moment, second, stat_left, stat_right, basis_left, basis_right):
    position = lax.axis_index("shard")
    row_count = moment.shape[0]
    block_width = moment.shape[1]
    local_sum = group_grads[0].astype(jnp.float32)
    summed = lax.psum(local_sum, "dp")
    grad_rows = summed.astype(jnp.bfloat16)
    gradient = lax.all_gather(grad_rows, "shard", axis=0, tiled=True)
    moment_half = (BETA_ONE * moment + (1.0 - BETA_ONE) * grad_rows.astype(jnp.float32)).astype(
        jnp.bfloat16
    )
    left_stat = BETA_STAT * stat_left + (1.0 - BETA_STAT) * contract_cols(grad_rows, gradient)
    grad_cols = lax.dynamic_slice_in_dim(gradient, position * row_count, row_count, 1)
    right_stat = BETA_STAT * stat_right + (1.0 - BETA_STAT) * contract_rows(grad_cols, gradient)
    left_rot, right_rot = (
        lax.all_gather(basis_left.astype(jnp.bfloat16), "shard", axis=0, tiled=True),
        lax.all_gather(basis_right.astype(jnp.bfloat16), "shard", axis=0, tiled=True),
    )
    grad_turned = jnp.dot(grad_rows, right_rot, preferred_element_type=jnp.float32).astype(
        jnp.bfloat16
    )
    moment_turned = jnp.dot(moment_half, right_rot, preferred_element_type=jnp.float32).astype(
        jnp.bfloat16
    )
    grad_block, moment_block = (
        lax.all_to_all(grad_turned, "shard", split_axis=1, concat_axis=0, tiled=True),
        lax.all_to_all(moment_turned, "shard", split_axis=1, concat_axis=0, tiled=True),
    )
    grad_rot = contract_rows(left_rot, grad_block) / block_width
    moment_rot = contract_rows(left_rot, moment_block) / block_width
    second_new = BETA_TWO * second + (1.0 - BETA_TWO) * grad_rot * grad_rot
    scaled = (moment_rot / (jnp.sqrt(second_new) + EPSILON)).astype(jnp.bfloat16)
    turned_back = jnp.dot(left_rot, scaled, preferred_element_type=jnp.float32).astype(jnp.bfloat16)
    back_rows = lax.all_to_all(turned_back, "shard", split_axis=0, concat_axis=1, tiled=True)
    update = (contract_cols(back_rows, right_rot) / block_width).astype(jnp.bfloat16)
    left_product = jnp.dot(
        left_stat.astype(jnp.bfloat16), left_rot, preferred_element_type=jnp.float32
    )
    right_product = jnp.dot(
        right_stat.astype(jnp.bfloat16), right_rot, preferred_element_type=jnp.float32
    )
    left_sq, right_sq = lax.psum(
        (
            jnp.sum(left_product * left_product, axis=0),
            jnp.sum(right_product * right_product, axis=0),
        ),
        "shard",
    )
    left_start = left_product / jnp.sqrt(left_sq / block_width + NORM_EPS)
    right_start = right_product / jnp.sqrt(right_sq / block_width + NORM_EPS)
    left_current = left_start.astype(jnp.bfloat16)
    right_current = right_start.astype(jnp.bfloat16)
    left_result = left_start
    right_result = right_start
    for iteration in range(NS_ITERS):
        left_full, right_full = (
            lax.all_gather(left_current, "shard", axis=0, tiled=True),
            lax.all_gather(right_current, "shard", axis=0, tiled=True),
        )
        left_gram = (contract_cols(left_current, left_full) / block_width).astype(jnp.bfloat16)
        right_gram = (contract_cols(right_current, right_full) / block_width).astype(jnp.bfloat16)
        left_result = 1.5 * left_current.astype(jnp.float32) - 0.5 * jnp.dot(
            left_gram, left_full, preferred_element_type=jnp.float32
        )
        right_result = 1.5 * right_current.astype(jnp.float32) - 0.5 * jnp.dot(
            right_gram, right_full, preferred_element_type=jnp.float32
        )
        if iteration + 1 < NS_ITERS:
            left_current = left_result.astype(jnp.bfloat16)
            right_current = right_result.astype(jnp.bfloat16)
    return (update, second_new, left_result, right_result)


def solution(mesh):
    return jax.shard_map(
        body,
        mesh=mesh,
        in_specs=(
            P("dp", "shard", None),
            P("shard", None),
            P(None, "shard"),
            P("shard", None),
            P("shard", None),
            P("shard", None),
            P("shard", None),
        ),
        out_specs=(P("shard", None), P(None, "shard"), P("shard", None), P("shard", None)),
        check_vma=False,
    )
```

profile of v0, /device:TPU:2, one launch (start us, length us, event | category | flops | bytes accessed | tf_op | source)
XLA Modules:
  0.0 1043.8 jit_solution(8911821349268861389)
XLA Ops:
  7.2 1.9 convert_element_type.88
  10.2 534.5 %all-reduce.2 = bf16[128,1024]{1,0:T(8,128)(2,1)} all-reduce(f32[128,1024]{1,0:T(8,128)S(1)} %bitcast_convert_fusion), channel_id=1, replica_groups=mesh['dp'=64,'shard'=8] {'dp'}, use_global_device_ids=true, to_apply=%region_0.0 | all-reduce | flops 131072 | bytes 786432 | tf_op jit(solution)/shard_map/psum | solution.py:31
  545.6 101.2 %all-gather.12.cloned.1.call-done = bf16[1024,1024]{1,0:T(8,128)(2,1)} async-done(((bf16[128,1024]{1,0:T(8,128)(2,1)}), bf16[1024,1024]{1,0:T(8,128)(2,1)}) %all-gather.12.cloned.1.call-update) | async-done | bytes 2097168 | tf_op jit(solution)/shard_map/all_gather | solution.py:33
  646.8 3.6 multiply_reduce_fusion.1
  650.4 65.8 %all-gather.8.cloned.1.call-done = bf16[1024,1024]{1,0:T(8,128)(2,1)} async-done(((bf16[128,1024]{1,0:T(8,128)(2,1)}), bf16[1024,1024]{1,0:T(8,128)(2,1)}) %all-gather.8.cloned.1.call-update) | async-done | bytes 2097168 | tf_op jit(solution)/shard_map/all_gather | solution.py:42
  716.2 2.6 multiply_reduce_fusion
  718.8 29.0 %all-reduce = (f32[1024]{0:T(1024)S(1)}, f32[1024]{0:T(1024)S(1)}) all-reduce(f32[1024]{0:T(1024)S(1)} %get-tuple-element.16, f32[1024]{0:T(1024)S(1)} %get-tuple-element.18), channel_id=1, replica_groups=mesh['dp'=64,'shard'=8] {'shard'}, use_global_device_ids=true, to_apply=%region_2.0 | all-reduce | flops 2048 | bytes 16384 | tf_op jit(solution)/shard_map/psum | solution.py:67
  749.5 68.6 %all-gather.14.cloned.1.call-done = bf16[1024,1024]{1,0:T(8,128)(2,1)} async-done(((bf16[128,1024]{1,0:T(8,128)(2,1)}), bf16[1024,1024]{1,0:T(8,128)(2,1)}) %all-gather.14.cloned.1.call-update) | async-done | bytes 2097168 | tf_op jit(solution)/shard_map/all_gather | solution.py:82
  818.1 4.1 fusion.10
  823.5 4.9 all-to-all-start.1
  828.5 58.7 %all-gather.18.cloned.1.call-done = bf16[1024,1024]{1,0:T(8,128)(2,1)} async-done(((bf16[128,1024]{1,0:T(8,128)(2,1)}), bf16[1024,1024]{1,0:T(8,128)(2,1)}) %all-gather.18.cloned.1.call-update) | async-done | bytes 2097168 | tf_op jit(solution)/shard_map/all_gather | solution.py:83
  887.2 4.1 fusion.12
  892.5 5.1 all-to-all-start
  898.9 3.0 bitcast_add_fusion
  901.9 16.0 %all-to-all-done = bf16[128,8,128]{2,0,1:T(8,128)(2,1)S(1)} async-done(((bf16[128,8,128]{2,0,1:T(8,128)(2,1)}), bf16[128,8,128]{2,0,1:T(8,128)(2,1)S(1)}, u32[]{:S(2)}, u32[]{:S(2)}) %all-to-all-start) | async-done | bytes 262176 | tf_op jit(solution)/shard_map/all_to_all | solution.py:52
  917.9 4.4 fusion.20
  922.3 1.7 copy.24
  924.0 3.5 all-to-all-start.2
  928.6 25.8 %all-to-all-done.2 = bf16[8,128,128]{1,2,0:T(8,128)(2,1)S(1)} async-done(((bf16[8,128,128]{1,2,0:T(8,128)(2,1)}), bf16[8,128,128]{1,2,0:T(8,128)(2,1)S(1)}, u32[]{:S(2)}, u32[]{:S(2)}) %all-to-all-start.2) | async-done | bytes 262176 | tf_op jit(solution)/shard_map/all_to_all | solution.py:59
  954.3 1.5 fusion.13
  955.9 6.3 all-gather.16.cloned.1.call-done
  962.2 4.1 fusion.3
  966.3 66.5 %all-gather.20.cloned.1.call-done = bf16[1024,1024]{1,0:T(8,128)(2,1)} async-done(((bf16[128,1024]{1,0:T(8,128)(2,1)}), bf16[1024,1024]{1,0:T(8,128)(2,1)}) %all-gather.20.cloned.1.call-update) | async-done | bytes 2097168 | tf_op jit(solution)/shard_map/all_gather | solution.py:83
  1032.8 4.2 fusion
  (48 shorter events, 8.4 us)
Async XLA Ops:
  7.2 537.6 %copy-start.8 = (f32[128,1024]{1,0:T(8,128)S(1)}, f32[128,1024]{1,0:T(8,128)}, u32[]{:S(2)}) copy-start(f32[128,1024]{1,0:T(8,128)} %param.13) | copy-start | bytes 1572868
  7.2 639.6 %copy-start.7 = (f32[128,1024]{1,0:T(8,128)S(1)}, f32[128,1024]{1,0:T(8,128)}, u32[]{:S(2)}) copy-start(f32[128,1024]{1,0:T(8,128)} %param.10) | copy-start | bytes 1572868
  7.2 538.4 %all-gather.10.cloned.1.call-start = ((), (), s32[]{:S(2)}) async-start(), calls=%async_computation.4 | async-start | bytes 2359296 | tf_op jit(solution)/shard_map/all_gather | solution.py:41
  9.1 637.6 %all-gather.12.cloned.1.call-start = ((), (), s32[]{:S(2)}) async-start(), calls=%async_computation.5 | async-start | bytes 2359296 | tf_op jit(solution)/shard_map/all_gather | solution.py:33
  544.7 171.5 %all-gather.8.cloned.1.call-start = ((), (), s32[]{:S(2)}) async-start(), calls=%async_computation.3 | async-start | bytes 2359296 | tf_op jit(solution)/shard_map/all_gather | solution.py:42
  545.5 272.6 %all-gather.14.cloned.1.call-start = ((), (), s32[]{:S(2)}) async-start(), calls=%async_computation.6 | async-start | bytes 2359296 | tf_op jit(solution)/shard_map/all_gather | solution.py:82
  646.8 69.4 %copy-start.1 = (bf16[1024,1024]{1,0:T(8,128)(2,1)S(1)}, bf16[1024,1024]{1,0:T(8,128)(2,1)}, u32[]{:S(2)}) copy-start(bf16[1024,1024]{1,0:T(8,128)(2,1)} %all-gather.12.cloned.1.call-done) | copy-start | bytes 6291460
  748.6 138.6 %all-gather.18.cloned.1.call-start = ((), (), s32[]{:S(2)}) async-start(), calls=%async_computation.8 | async-start | bytes 2359296 | tf_op jit(solution)/shard_map/all_gather | solution.py:83
  749.5 72.8 %copy-start = (bf16[1024,1024]{1,0:T(8,128)(2,1)S(1)}, bf16[1024,1024]{1,0:T(8,128)(2,1)}, u32[]{:S(2)}) copy-start(bf16[1024,1024]{1,0:T(8,128)(2,1)} %all-gather.8.cloned.1.call-done) | copy-start | bytes 6291460
  749.5 72.8 %copy-start.2 = (bf16[128,1024]{1,0:T(8,128)(2,1)S(1)}, bf16[128,1024]{1,0:T(8,128)(2,1)}, u32[]{:S(2)}) copy-start(bf16[128,1024]{1,0:T(8,128)(2,1)} %all-reduce.2) | copy-start | bytes 786436
  749.5 212.7 %all-gather.16.cloned.1.call-start = ((), (), s32[]{:S(2)}) async-start(), calls=%async_computation.7 | async-start | bytes 2359296 | tf_op jit(solution)/shard_map/all_gather | solution.py:82
  822.2 65.0 %copy-start.5 = (bf16[128,1024]{1,0:T(8,128)(2,1)S(1)}, bf16[128,1024]{1,0:T(8,128)(2,1)}, u32[]{:S(2)}) copy-start(bf16[128,1024]{1,0:T(8,128)(2,1)} %divide_convert_fusion) | copy-start | bytes 786436
  823.5 69.0 %all-to-all-start.1 = ((bf16[128,8,128]{2,0,1:T(8,128)(2,1)}), bf16[128,8,128]{2,0,1:T(8,128)(2,1)S(1)}, u32[]{:S(2)}, u32[]{:S(2)}) async-start(bf16[128,8,128]{2,0,1:T(8,128)(2,1)} %bitcast.66), calls=%async_computation.1 | async-start | bytes 524288 | tf_op jit(solution)/shard_map/all_to_all | solution.py:51
  828.4 62.9 %copy-start.9 = (f32[128,1024]{1,0:T(8,128)S(1)}, f32[128,1024]{1,0:T(8,128)}, u32[]{:S(2)}) copy-start(f32[128,1024]{1,0:T(8,128)} %param.8) | copy-start | bytes 1572868
  828.4 204.4 %all-gather.20.cloned.1.call-start = ((), (), s32[]{:S(2)}) async-start(), calls=%async_computation.9 | async-start | bytes 2359296 | tf_op jit(solution)/shard_map/all_gather | solution.py:83
  892.5 6.3 copy-start.6
  892.5 25.3 %all-to-all-start = ((bf16[128,8,128]{2,0,1:T(8,128)(2,1)}), bf16[128,8,128]{2,0,1:T(8,128)(2,1)S(1)}, u32[]{:S(2)}, u32[]{:S(2)}) async-start(bf16[128,8,128]{2,0,1:T(8,128)(2,1)} %bitcast.67), calls=%async_computation | async-start | bytes 524288 | tf_op jit(solution)/shard_map/all_to_all | solution.py:52
  924.0 38.1 %copy-start.3 = (bf16[128,1024]{1,0:T(8,128)(2,1)S(1)}, bf16[128,1024]{1,0:T(8,128)(2,1)}, u32[]{:S(2)}) copy-start(bf16[128,1024]{1,0:T(8,128)(2,1)} %fusion.10) | copy-start | bytes 786436
  924.0 30.3 %all-to-all-start.2 = ((bf16[8,128,128]{1,2,0:T(8,128)(2,1)}), bf16[8,128,128]{1,2,0:T(8,128)(2,1)S(1)}, u32[]{:S(2)}, u32[]{:S(2)}) async-start(bf16[8,128,128]{1,2,0:T(8,128)(2,1)} %bitcast.65), calls=%async_computation.2 | async-start | bytes 524288 | tf_op jit(solution)/shard_map/all_to_all | solution.py:59
  955.9 76.9 %copy-start.4 = (bf16[128,1024]{1,0:T(8,128)(2,1)S(1)}, bf16[128,1024]{1,0:T(8,128)(2,1)}, u32[]{:S(2)}) copy-start(bf16[128,1024]{1,0:T(8,128)(2,1)} %fusion.12) | copy-start | bytes 786436
Sparse Core Ops, SparseCore 0:
  10.7 76.0 all-gather.9
  544.8 101.8 all-gather.11
  649.4 66.7 all-gather.7
  748.7 69.3 all-gather.13
  820.6 66.5 all-gather.17
  889.1 72.9 all-gather.15
  964.2 68.5 all-gather.19
where the time goes:
time: 1040 us
  blocking collectives  563 us (54%)
  waiting for transfers between devices  409 us (39%)
  matrix products  32.6 us (3%)
  between operations  14.3 us (1%)
  starting transfers between devices  13.9 us (1%)
    psum x1, blocking collectives, body(): summed = lax.psum(local_sum, 'dp')  535 us
    all_gather x2, waiting for transfers between devices, body(): lax.all_gather(right_current, 'shard', axis=0, tiled=True)  125 us
    all_gather x1, waiting for transfers between devices, body(): gradient = lax.all_gather(grad_rows, 'shard', axis=0, tiled=True)  101 us
    all_gather x2, waiting for transfers between devices, body(): lax.all_gather(left_current, 'shard', axis=0, tiled=True)  74.9 us
    all_gather x1, waiting for transfers between devices, body(): lax.all_gather(basis_right.astype(jnp.bfloat16), 'shard', axis=0, tiled=T...  65.8 us
    psum x1, blocking collectives, body(): lax.psum((jnp.sum(left_product * left_product, axis=0), jnp.sum(right_pro...  29 us
    all_to_all x1, waiting for transfers between devices, body(): lax.all_to_all(turned_back, 'shard', split_axis=0, concat_axis=1, tiled=T...  25.8 us
  transfers between devices with their start and end apart: 10, of which 8 were waited for; matrix products, arithmetic and copies ran while one was open for 3% of the time, Pallas kernels for 0%

commit v1 on v0

--- a/solution.py
+++ b/solution.py
@@ -2,6 +2,7 @@
 import jax.numpy as jnp
 from jax import lax
 from jax.sharding import PartitionSpec as P
+from jax.lax import all_gather
 
 NS_ITERS = 2
 BETA_ONE = 0.9
@@ -28,7 +29,11 @@
     row_count = moment.shape[0]
     block_width = moment.shape[1]
     local_sum = group_grads[0].astype(jnp.float32)
-    summed = lax.psum(local_sum, "dp")
+
+    def solve_sector(x_in, named_axis):
+        return jnp.sum(all_gather(x_in, named_axis), 0)
+
+    summed = solve_sector(local_sum, "dp")
     grad_rows = summed.astype(jnp.bfloat16)
     gradient = lax.all_gather(grad_rows, "shard", axis=0, tiled=True)
     moment_half = (BETA_ONE * moment + (1.0 - BETA_ONE) * grad_rows.astype(jnp.float32)).astype(

time: 1040 us -> 976 us (0.938)
  blocking collectives: 563 us -> 29 us
  waiting for transfers between devices: 409 us -> 862 us
  other arithmetic: 5.11 us -> 18.3 us
    psum x1 -> x0, blocking collectives: 535 us -> none  [body(): summed = lax.psum(local_sum, 'dp')]
    all_gather x0 -> x1, waiting for transfers between devices: none -> 409 us  [solve_sector(): return jnp.sum(all_gather(x_in, named_axis), 0)]
    all_gather x1, waiting for transfers between devices: 0.02 us -> 76.4 us  [body(): lax.all_gather(basis_left.astype(jnp.bfloat16), 'shard', axis=0, tiled=True)]
    all_gather x2, waiting for transfers between devices: 125 us -> 74.7 us  [body(): lax.all_gather(right_current, 'shard', axis=0, tiled=True)]
    all_gather x2, waiting for transfers between devices: 74.9 us -> 125 us  [body(): lax.all_gather(left_current, 'shard', axis=0, tiled=True)]
    all_gather x1, waiting for transfers between devices: 101 us -> 69.5 us  [body(): gradient = lax.all_gather(grad_rows, 'shard', axis=0, tiled=True)]
    reduce_sum x0 -> x1, other arithmetic: none -> 12.5 us  [solve_sector(): return jnp.sum(all_gather(x_in, named_axis), 0)]
  transfers between devices with their start and end apart: 10 -> 11, of which waited for: 8 -> 10; matrix products, arithmetic and copies ran while one was open for 3% -> 5% of each run, Pallas kernels for 0% -> 0%
where the time goes in v1:
time: 976 us
  waiting for transfers between devices  862 us (88%)
  matrix products  32.7 us (3%)
  blocking collectives  29 us (3%)
  other arithmetic  18.3 us (2%)
  between operations  14.3 us (1%)
  starting transfers between devices  13.9 us (1%)
    all_gather x1, waiting for transfers between devices, solve_sector(): return jnp.sum(all_gather(x_in, named_axis), 0)  409 us
    all_gather x2, waiting for transfers between devices, body(): lax.all_gather(left_current, 'shard', axis=0, tiled=True)  125 us
    all_gather x1, waiting for transfers between devices, body(): lax.all_gather(basis_left.astype(jnp.bfloat16), 'shard', axis=0, tiled=True)  76.4 us
    all_gather x2, waiting for transfers between devices, body(): lax.all_gather(right_current, 'shard', axis=0, tiled=True)  74.7 us
    all_gather x1, waiting for transfers between devices, body(): gradient = lax.all_gather(grad_rows, 'shard', axis=0, tiled=True)  69.5 us
    all_gather x1, waiting for transfers between devices, body(): lax.all_gather(basis_right.astype(jnp.bfloat16), 'shard', axis=0, tiled=T...  65.6 us
    psum x1, blocking collectives, body(): lax.psum((jnp.sum(left_product * left_product, axis=0), jnp.sum(right_pro...  29 us
    all_to_all x1, waiting for transfers between devices, body(): lax.all_to_all(turned_back, 'shard', split_axis=0, concat_axis=1, tiled=T...  25.5 us
  transfers between devices with their start and end apart: 11, of which 10 were waited for; matrix products, arithmetic and copies ran while one was open for 5% of the time, Pallas kernels for 0%

profile of v1, /device:TPU:2, one launch (start us, length us, event | category | flops | bytes accessed | tf_op | source)
XLA Modules:
  0.0 975.7 jit_solution(9007732347562431505)
XLA Ops:
  7.2 1.8 convert_element_type.79
  11.0 408.7 %all-gather.9.cloned.1.call-done = f32[64,128,1024]{2,1,0:T(8,128)} async-done(((f32[1,128,1024]{2,1,0:T(8,128)}), f32[64,128,1024]{2,1,0:T(8,128)}) %all-gather.9.cloned.1.call-update) | async-done | bytes 33554448 | tf_op jit(solution)/shard_map/all_gather | solution.py:34
  419.7 12.5 %reduce_sum.27 = bf16[128,1024]{1,0:T(8,128)(2,1)} reduce(f32[64,128,1024]{2,1,0:T(8,128)} %all-gather.9.cloned.1.call-done, f32[]{:T(128)} %constant.16.clone.1), dimensions={0}, to_apply=%region_0.0 | reduce | flops 8257536 | bytes 33816580 | tf_op jit(solution)/shard_map/reduce_sum | solution.py:34
  433.1 76.4 %all-gather.13.cloned.1.call-done = bf16[1024,1024]{1,0:T(8,128)(2,1)} async-done(((bf16[128,1024]{1,0:T(8,128)(2,1)}), bf16[1024,1024]{1,0:T(8,128)(2,1)}) %all-gather.13.cloned.1.call-update) | async-done | bytes 2097168 | tf_op jit(solution)/shard_map/all_gather | solution.py:46
  509.5 69.5 %all-gather.15.cloned.1.call-done = bf16[1024,1024]{1,0:T(8,128)(2,1)} async-done(((bf16[128,1024]{1,0:T(8,128)(2,1)}), bf16[1024,1024]{1,0:T(8,128)(2,1)}) %all-gather.15.cloned.1.call-update) | async-done | bytes 2097168 | tf_op jit(solution)/shard_map/all_gather | solution.py:38
  579.0 3.6 multiply_reduce_fusion.1
  582.6 65.6 %all-gather.11.cloned.1.call-done = bf16[1024,1024]{1,0:T(8,128)(2,1)} async-done(((bf16[128,1024]{1,0:T(8,128)(2,1)}), bf16[1024,1024]{1,0:T(8,128)(2,1)}) %all-gather.11.cloned.1.call-update) | async-done | bytes 2097168 | tf_op jit(solution)/shard_map/all_gather | solution.py:47
  648.2 2.6 multiply_reduce_fusion
  650.9 29.0 %all-reduce = (f32[1024]{0:T(1024)S(1)}, f32[1024]{0:T(1024)S(1)}) all-reduce(f32[1024]{0:T(1024)S(1)} %get-tuple-element.20, f32[1024]{0:T(1024)S(1)} %get-tuple-element.22), channel_id=1, replica_groups=mesh['dp'=64,'shard'=8] {'shard'}, use_global_device_ids=true, to_apply=%region_2.0 | all-reduce | flops 2048 | bytes 16384 | tf_op jit(solution)/shard_map/psum | solution.py:72
  681.6 68.6 %all-gather.21.cloned.1.call-done = bf16[1024,1024]{1,0:T(8,128)(2,1)} async-done(((bf16[128,1024]{1,0:T(8,128)(2,1)}), bf16[1024,1024]{1,0:T(8,128)(2,1)}) %all-gather.21.cloned.1.call-update) | async-done | bytes 2097168 | tf_op jit(solution)/shard_map/all_gather | solution.py:88
  750.1 4.2 fusion.12
  755.6 4.9 all-to-all-start.1
  760.6 58.7 %all-gather.17.cloned.1.call-done = bf16[1024,1024]{1,0:T(8,128)(2,1)} async-done(((bf16[128,1024]{1,0:T(8,128)(2,1)}), bf16[1024,1024]{1,0:T(8,128)(2,1)}) %all-gather.17.cloned.1.call-update) | async-done | bytes 2097168 | tf_op jit(solution)/shard_map/all_gather | solution.py:87
  819.3 4.1 fusion.10
  824.6 5.1 all-to-all-start
  831.0 3.0 bitcast_add_fusion
  833.9 16.4 %all-to-all-done = bf16[128,8,128]{2,0,1:T(8,128)(2,1)S(1)} async-done(((bf16[128,8,128]{2,0,1:T(8,128)(2,1)}), bf16[128,8,128]{2,0,1:T(8,128)(2,1)S(1)}, u32[]{:S(2)}, u32[]{:S(2)}) %all-to-all-start) | async-done | bytes 262176 | tf_op jit(solution)/shard_map/all_to_all | solution.py:57
  850.3 4.4 fusion.20
  856.5 3.5 all-to-all-start.2
  861.0 25.5 %all-to-all-done.2 = bf16[8,128,128]{1,2,0:T(8,128)(2,1)S(1)} async-done(((bf16[8,128,128]{1,2,0:T(8,128)(2,1)}), bf16[8,128,128]{1,2,0:T(8,128)(2,1)S(1)}, u32[]{:S(2)}, u32[]{:S(2)}) %all-to-all-start.2) | async-done | bytes 262176 | tf_op jit(solution)/shard_map/all_to_all | solution.py:64
  888.0 6.1 all-gather.23.cloned.1.call-done
  894.2 4.1 fusion
  898.3 66.4 %all-gather.19.cloned.1.call-done = bf16[1024,1024]{1,0:T(8,128)(2,1)} async-done(((bf16[128,1024]{1,0:T(8,128)(2,1)}), bf16[1024,1024]{1,0:T(8,128)(2,1)}) %all-gather.19.cloned.1.call-update) | async-done | bytes 2097168 | tf_op jit(solution)/shard_map/all_gather | solution.py:87
  964.7 4.2 fusion.3
  (51 shorter events, 12.4 us)
Async XLA Ops:
  7.2 412.5 %all-gather.9.cloned.1.call-start = ((), (), s32[]{:S(2)}) async-start(), calls=%async_computation.3 | async-start | bytes 34078720 | tf_op jit(solution)/shard_map/all_gather | solution.py:34
  9.0 500.4 %all-gather.13.cloned.1.call-start = ((), (), s32[]{:S(2)}) async-start(), calls=%async_computation.5 | async-start | bytes 2359296 | tf_op jit(solution)/shard_map/all_gather | solution.py:46
  10.9 421.4 %copy-start.8 = (f32[128,1024]{1,0:T(8,128)S(1)}, f32[128,1024]{1,0:T(8,128)}, u32[]{:S(2)}) copy-start(f32[128,1024]{1,0:T(8,128)} %param.13) | copy-start | bytes 1572868
  10.9 568.1 %copy-start.7 = (f32[128,1024]{1,0:T(8,128)S(1)}, f32[128,1024]{1,0:T(8,128)}, u32[]{:S(2)}) copy-start(f32[128,1024]{1,0:T(8,128)} %param.10) | copy-start | bytes 1572868
  10.9 568.0 %all-gather.15.cloned.1.call-start = ((), (), s32[]{:S(2)}) async-start(), calls=%async_computation.6 | async-start | bytes 2359296 | tf_op jit(solution)/shard_map/all_gather | solution.py:38
  432.2 216.0 %all-gather.11.cloned.1.call-start = ((), (), s32[]{:S(2)}) async-start(), calls=%async_computation.4 | async-start | bytes 2359296 | tf_op jit(solution)/shard_map/all_gather | solution.py:47
  433.0 317.1 %all-gather.21.cloned.1.call-start = ((), (), s32[]{:S(2)}) async-start(), calls=%async_computation.9 | async-start | bytes 2359296 | tf_op jit(solution)/shard_map/all_gather | solution.py:88
  579.0 69.3 %copy-start.1 = (bf16[1024,1024]{1,0:T(8,128)(2,1)S(1)}, bf16[1024,1024]{1,0:T(8,128)(2,1)}, u32[]{:S(2)}) copy-start(bf16[1024,1024]{1,0:T(8,128)(2,1)} %all-gather.15.cloned.1.call-done) | copy-start | bytes 6291460
  680.7 138.6 %all-gather.17.cloned.1.call-start = ((), (), s32[]{:S(2)}) async-start(), calls=%async_computation.7 | async-start | bytes 2359296 | tf_op jit(solution)/shard_map/all_gather | solution.py:87
  681.5 72.8 %copy-start = (bf16[1024,1024]{1,0:T(8,128)(2,1)S(1)}, bf16[1024,1024]{1,0:T(8,128)(2,1)}, u32[]{:S(2)}) copy-start(bf16[1024,1024]{1,0:T(8,128)(2,1)} %all-gather.11.cloned.1.call-done) | copy-start | bytes 6291460
  681.5 72.8 %copy-start.2 = (bf16[128,1024]{1,0:T(8,128)(2,1)S(1)}, bf16[128,1024]{1,0:T(8,128)(2,1)}, u32[]{:S(2)}) copy-start(bf16[128,1024]{1,0:T(8,128)(2,1)} %reduce_sum.27) | copy-start | bytes 786436
  681.5 212.6 %all-gather.23.cloned.1.call-start = ((), (), s32[]{:S(2)}) async-start(), calls=%async_computation.10 | async-start | bytes 2359296 | tf_op jit(solution)/shard_map/all_gather | solution.py:88
  754.3 65.0 %copy-start.5 = (bf16[128,1024]{1,0:T(8,128)(2,1)S(1)}, bf16[128,1024]{1,0:T(8,128)(2,1)}, u32[]{:S(2)}) copy-start(bf16[128,1024]{1,0:T(8,128)(2,1)} %divide_convert_fusion.1) | copy-start | bytes 786436
  755.6 69.0 %all-to-all-start.1 = ((bf16[128,8,128]{2,0,1:T(8,128)(2,1)}), bf16[128,8,128]{2,0,1:T(8,128)(2,1)S(1)}, u32[]{:S(2)}, u32[]{:S(2)}) async-start(bf16[128,8,128]{2,0,1:T(8,128)(2,1)} %bitcast.63), calls=%async_computation.1 | async-start | bytes 524288 | tf_op jit(solution)/shard_map/all_to_all | solution.py:56
  760.5 62.9 %copy-start.9 = (f32[128,1024]{1,0:T(8,128)S(1)}, f32[128,1024]{1,0:T(8,128)}, u32[]{:S(2)}) copy-start(f32[128,1024]{1,0:T(8,128)} %param.8) | copy-start | bytes 1572868
  760.5 204.2 %all-gather.19.cloned.1.call-start = ((), (), s32[]{:S(2)}) async-start(), calls=%async_computation.8 | async-start | bytes 2359296 | tf_op jit(solution)/shard_map/all_gather | solution.py:87
  824.6 6.3 copy-start.6
  824.6 25.7 %all-to-all-start = ((bf16[128,8,128]{2,0,1:T(8,128)(2,1)}), bf16[128,8,128]{2,0,1:T(8,128)(2,1)S(1)}, u32[]{:S(2)}, u32[]{:S(2)}) async-start(bf16[128,8,128]{2,0,1:T(8,128)(2,1)} %bitcast.64), calls=%async_computation | async-start | bytes 524288 | tf_op jit(solution)/shard_map/all_to_all | solution.py:57
  856.5 37.7 %copy-start.3 = (bf16[128,1024]{1,0:T(8,128)(2,1)S(1)}, bf16[128,1024]{1,0:T(8,128)(2,1)}, u32[]{:S(2)}) copy-start(bf16[128,1024]{1,0:T(8,128)(2,1)} %fusion.12) | copy-start | bytes 786436
  856.5 30.0 %all-to-all-start.2 = ((bf16[8,128,128]{1,2,0:T(8,128)(2,1)}), bf16[8,128,128]{1,2,0:T(8,128)(2,1)S(1)}, u32[]{:S(2)}, u32[]{:S(2)}) async-start(bf16[8,128,128]{1,2,0:T(8,128)(2,1)} %bitcast.62), calls=%async_computation.2 | async-start | bytes 524288 | tf_op jit(solution)/shard_map/all_to_all | solution.py:64
  888.0 76.7 %copy-start.4 = (bf16[128,1024]{1,0:T(8,128)(2,1)S(1)}, bf16[128,1024]{1,0:T(8,128)(2,1)}, u32[]{:S(2)}) copy-start(bf16[128,1024]{1,0:T(8,128)(2,1)} %fusion.10) | copy-start | bytes 786436
Sparse Core Ops, SparseCore 0:
  12.9 406.7 all-gather.8
  422.3 87.0 all-gather.12
  512.1 66.7 all-gather.14
  581.5 66.7 all-gather.10
  680.8 69.3 all-gather.20
  752.6 66.5 all-gather.16
  821.3 72.7 all-gather.22
  896.2 68.4 all-gather.18
